TPU v7x, 1024 devices: a whole 4x8x16 slice. The times are simulated.
1024 devices in a mesh: ctx: 64 (over y, z_hi, core), ch: 16 (over z_lo, x).
Axes of the slice: x: 4, y: 8, z: 16 (z_hi: 4, z_lo: 4; z = z_hi * 4 + z_lo), core: 2. Of those that a mesh axis runs over, the one named last changes fastest.
Arguments:
- q_mr: bfloat16 [1024, 32768], P('ch', 'ctx'), may hold values from -6 to 6
- k_mr: bfloat16 [1024, 32768], P('ch', 'ctx'), may hold values from -6 to 6
- v_mr: bfloat16 [1024, 32768], P('ch', 'ctx'), may hold values from -22 to 22
- mr_taps: bfloat16 [128, 1024], P(None, 'ch'), may hold values from -0.5 to 0.5
- norm_gain: float32 [1024], P('ch'), may hold values from 0.5 to 1.5
- q_li: bfloat16 [1024, 32768], P('ch', 'ctx'), may hold values from -6 to 6
- k_li: bfloat16 [1024, 32768], P('ch', 'ctx'), may hold values from -6 to 6
- rates: float32 [1024, 16], P('ch'), may hold values from 9.1552734e-06 to 0.0333333333, as said below
- residues: float32 [1024, 16], P('ch'), may hold values from -2 to 2
- skip: float32 [1024], P('ch'), may hold values from 0.5 to 1.5
Outputs:
- mixed: bfloat16 [1024, 32768], P('ch', 'ctx')
Inputs may be any that keep to these rules, and one draw needn't show every extreme that they name: Positive decay rates.
All inputs are finite; a program needn't handle non-finite values.
Results may differ from a plain program's by a relative error of at most 0.0085.
Values may be sent and summed in bfloat16 or wider, within the bound.
A program may use at most 32 MiB of HBM per device.

v0:
```python
import jax
import jax.numpy as jnp
from jax import lax
from jax.sharding import PartitionSpec as P

CH = 1024


def shifted(block, axis, distance):
    devices = range(lax.axis_size(axis))
    route = [(i - distance, i) for i in devices if i - distance in devices]
    return lax.ppermute(block, axis, route)


def banded(column, offset):
    width = column.shape[1]
    lag = jnp.arange(width)[:, None] - jnp.arange(width)[None, :] + offset
    valid = (lag >= 0) & (lag < width)
    table = column[:, jnp.clip(lag, 0, width - 1)]
    return jnp.where(valid[None, :, :], table, jnp.zeros((), column.dtype))


def combine(early, late):
    return (early[0] * late[0], early[1] * late[0] + late[1])


def modal_terms(signal, rate_part, residue_part, width):
    lanes, length = signal.shape
    count = length // width
    series = signal.astype(jnp.float32).reshape(lanes, count, width)
    offsets = jnp.arange(width, dtype=jnp.float32)
    powers = jnp.exp(-rate_part[:, :, None] * offsets[None, None, :])
    weight = residue_part * jnp.sqrt(rate_part)
    head = jnp.sum(powers * weight[:, :, None], axis=1)
    near = banded(head, 0)
    inner = jnp.einsum("cij,cnj->cni", near, series, precision=lax.Precision.HIGHEST)
    ends = jnp.einsum("cri,cni->ncr", powers[:, :, ::-1], series, precision=lax.Precision.HIGHEST)
    stride = jnp.broadcast_to(jnp.exp(-rate_part * width)[None], ends.shape)
    decays, states = lax.associative_scan(combine, (stride, ends), axis=0)
    before = jnp.concatenate([jnp.zeros_like(states[:1]), states[:-1]], axis=0)
    lift = powers * (jnp.exp(-rate_part) * weight)[:, :, None]
    return (inner, before, states[-1], lift)


def finish(signal, inner, before, lift, skip_part):
    lanes, length = signal.shape
    carried = jnp.einsum("cri,ncr->cni", lift, before, precision=lax.Precision.HIGHEST)
    result = (inner + carried).reshape(lanes, length) + skip_part[:, None] * signal.astype(
        jnp.float32
    )
    return result.astype(jnp.bfloat16)


def per_device(q_mr, k_mr, v_mr, mr_taps, norm_gain, q_li, k_li, rates, residues, skip):
    chans, rows = k_mr.shape
    width = mr_taps.shape[0]
    count = rows // width
    a_mr = (k_mr.astype(jnp.float32) * v_mr.astype(jnp.float32)).astype(jnp.bfloat16)
    blocks = a_mr.reshape(chans, count, width)
    rim = shifted(blocks[:, count - 1, :], "ctx", 1)
    tap_rows = mr_taps.T
    near = banded(tap_rows, 0)
    far = banded(tap_rows, width)
    inner = jnp.einsum("cij,cnj->cni", near, blocks, preferred_element_type=jnp.float32)
    later = jnp.einsum("cij,cnj->cni", far, blocks[:, :-1, :], preferred_element_type=jnp.float32)
    first = jnp.einsum("cij,cj->ci", far, rim, preferred_element_type=jnp.float32)
    mr_out = inner + jnp.concatenate([first[:, None, :], later], axis=1)
    gated = q_mr.astype(jnp.float32) * mr_out.reshape(chans, rows)
    total = lax.psum(jnp.sum(gated * gated, axis=0), "ch")
    inv_rms = lax.rsqrt(total / CH + 1e-05)
    v_li = (k_li.astype(jnp.float32) * gated * inv_rms[None, :] * norm_gain[:, None]).astype(
        jnp.bfloat16
    )
    lanes = chans // lax.axis_size("ctx")
    start = lax.axis_index("ctx") * lanes
    own_rates = lax.dynamic_slice_in_dim(rates, start, lanes, 0)
    own_residues = lax.dynamic_slice_in_dim(residues, start, lanes, 0)
    own_skip = lax.dynamic_slice_in_dim(skip, start, lanes, 0)
    whole = lax.all_to_all(v_li, "ctx", split_axis=0, concat_axis=1, tiled=True)
    inner_li, before, last_state, lift = modal_terms(whole, own_rates, own_residues, width)
    owned = finish(whole, inner_li, before, lift, own_skip)
    long_out = lax.all_to_all(owned, "ctx", split_axis=1, concat_axis=0, tiled=True)
    return (q_li.astype(jnp.float32) * long_out.astype(jnp.float32)).astype(jnp.bfloat16)


def solution(mesh):
    placed = (
        P("ch", "ctx"),
        P("ch", "ctx"),
        P("ch", "ctx"),
        P(None, "ch"),
        P("ch"),
        P("ch", "ctx"),
        P("ch", "ctx"),
        P("ch", None),
        P("ch", None),
        P("ch"),
    )
    return jax.shard_map(
        per_device, mesh=mesh, in_specs=placed, out_specs=P("ch", "ctx"), check_vma=False
    )
```

profile of v0, /device:TPU:56, one launch (start us, length us, event | category | flops | bytes accessed | tf_op | source)
XLA Modules:
  0.0 344.2 jit_solution(3451056560682886001)
XLA Ops:
  0.0 0.9 multiply_convert_fusion.1
  1.0 1.9 collective-permute-start
  3.0 0.8 copy.54
  3.8 57.4 %gather_fusion.1 = bf16[16384,64]{1,0:T(8,128)(2,1)} fusion(bf16[64,128]{0,1:T(8,128)(2,1)S(1)} %bitcast.90, s32[16384]{0:T(1024)S(1)} %fusion.17), kind=kCustom, calls=%fused_computation.1 | custom fusion | bytes 4259840 | tf_op jit(solution)/shard_map/gather | solution.py:19
  61.2 4.8 %copy.56 = bf16[128,128,64]{1,0,2:T(8,128)(2,1)S(1)} copy(bf16[128,128,64]{2,1,0:T(8,128)(2,1)} %bitcast.92) | data formatting | bytes 4194304 | tf_op jit(solution)/shard_map/gather | solution.py:19
  66.0 1.2 fusion
  67.2 0.3 fusion.50
  67.6 57.4 %gather_fusion = bf16[16384,64]{1,0:T(8,128)(2,1)} fusion(bf16[64,128]{0,1:T(8,128)(2,1)S(1)} %bitcast.91, s32[16384]{0:T(1024)S(1)} %fusion.15), kind=kCustom, calls=%fused_computation | custom fusion | bytes 4259840 | tf_op jit(solution)/shard_map/gather | solution.py:19
  125.0 5.6 %copy.55 = bf16[128,128,64]{1,0,2:T(8,128)(2,1)} copy(bf16[128,128,64]{2,1,0:T(8,128)(2,1)} %bitcast.93) | data formatting | bytes 4194304 | tf_op jit(solution)/shard_map/gather | solution.py:19
  130.6 1.2 fusion.2
  131.8 0.4 copy-done
  132.2 1.2 maximum_add_fusion
  133.4 46.0 %psum.7 = f32[512]{0:T(512)S(1)} all-reduce(f32[512]{0:T(512)S(1)} %multiply_reduce_fusion), channel_id=1, replica_groups=mesh['ctx'=64,'ch'=16] {'ch'}, use_global_device_ids=true, to_apply=%region_1.2 | all-reduce | flops 512 | bytes 4096 | tf_op jit(solution)/shard_map/psum | solution.py:69
  179.5 0.6 broadcast.430
  180.1 0.7 reduce.10
  180.8 0.6 reshape.475
  181.5 21.9 %all-to-all-start = ((bf16[64,2,256]{2,1,0:T(2,128)(2,1)}), bf16[64,2,256]{2,1,0:T(2,128)(2,1)S(1)}, u32[]{:S(2)}, u32[]{:S(2)}) async-start(bf16[64,2,256]{2,1,0:T(2,128)(2,1)} %reshape.475), calls=%async_computation | async-start | bytes 131072 | tf_op jit(solution)/shard_map/all_to_all | solution.py:79
  203.4 97.2 %gather_fusion.2 = f32[16384]{0:T(1024)S(1)} fusion(f32[128]{0:T(128)S(1)} %get-tuple-element.16, s32[16384]{0:T(1024)S(1)} %fusion.15), kind=kCustom, calls=%fused_computation.2 | custom fusion | bytes 196608 | tf_op jit(solution)/shard_map/gather | solution.py:19
  300.7 0.6 dynamic_slice.11
  301.4 0.4 reduce.1
  302.0 0.4 slice.179
  302.4 0.3 slice.181
  302.8 0.2 slice.183
  305.6 0.3 slice.227
  308.2 0.3 pad.108
  308.7 0.3 pad.86
  309.0 0.5 fusion.36
  309.5 0.2 convolution_add_fusion
  309.7 0.8 fusion.62
  310.5 1.1 reduce.11
  311.6 31.7 %all_to_all.23 = bf16[64,2,256]{2,1,0:T(2,128)(2,1)S(1)} all-to-all(bf16[64,2,256]{2,1,0:T(2,128)(2,1)S(1)} %reshape.477), channel_id=1, replica_groups=mesh['ctx'=64,'ch'=16] {'ctx'}, dimensions={0} | all-to-all | bytes 131072 | tf_op jit(solution)/shard_map/all_to_all | solution.py:82
  343.5 0.6 fusion.11
  (97 shorter events, 6.0 us)
Async XLA Ops:
  1.0 129.6 %collective-permute-start = (bf16[64,128]{1,0:T(8,128)(2,1)S(1)}, bf16[64,128]{1,0:T(8,128)(2,1)S(1)}, u32[]{:S(2)}, u32[]{:S(2)}) collective-permute-start(bf16[64,128]{1,0:T(8,128)(2,1)S(1)} %bitcast.106), channel_id=1, source_target_pairs={{0,16},{16,32},{32,48},{48,64},{64,80},{80,96},{96,112},{112,128},... | collective-permute-start | bytes 49160 | tf_op jit(solution)/shard_map/ppermute | solution.py:12
  66.0 1.2 copy-start.2
  66.0 1.2 copy-start.5
  130.6 1.6 copy-start
  132.2 1.2 copy-start.1
  132.2 47.2 %copy-start.3 = (bf16[64,512]{1,0:T(8,128)(2,1)S(1)}, bf16[64,512]{1,0:T(8,128)(2,1)}, u32[]{:S(2)}) copy-start(bf16[64,512]{1,0:T(8,128)(2,1)} %param.16) | copy-start | bytes 196612
  132.2 47.2 %copy-start.6 = (f32[64]{0:T(128)S(1)}, f32[64]{0:T(128)}, u32[]{:S(2)}) copy-start(f32[64]{0:T(128)} %param.14) | copy-start | bytes 772
  181.5 119.9 %all-to-all-start = ((bf16[64,2,256]{2,1,0:T(2,128)(2,1)}), bf16[64,2,256]{2,1,0:T(2,128)(2,1)S(1)}, u32[]{:S(2)}, u32[]{:S(2)}) async-start(bf16[64,2,256]{2,1,0:T(2,128)(2,1)} %reshape.475), calls=%async_computation | async-start | bytes 131072 | tf_op jit(solution)/shard_map/all_to_all | solution.py:79
  203.4 97.2 %copy-start.7 = (f32[64]{0:T(128)S(1)}, f32[64]{0:T(128)}, u32[]{:S(2)}) copy-start(f32[64]{0:T(128)} %param.19) | copy-start | bytes 772
  300.7 42.9 %copy-start.4 = (bf16[64,512]{1,0:T(8,128)(2,1)S(1)}, bf16[64,512]{1,0:T(8,128)(2,1)}, u32[]{:S(2)}) copy-start(bf16[64,512]{1,0:T(8,128)(2,1)} %param.15) | copy-start | bytes 196612
where the time goes:
time: 349 us; the launch traced here: 344 us
  local copies, waits for them, and re-layouts  231 us (66%)
  blocking collectives  77.7 us (22%)
  starting transfers between devices  23.8 us (7%)
  other arithmetic  7.12 us (2%)
  matrix products  4.34 us (1%)
    gather x5, local copies, waits for them, and re-layouts, banded(): table = column[:, jnp.clip(lag, 0, width - 1)]  222 us
    psum x1, blocking collectives, per_device(): total = lax.psum(jnp.sum(gated * gated, axis=0), 'ch')  46 us
    all_to_all x1, blocking collectives, per_device(): lax.all_to_all(owned, 'ctx', split_axis=1, concat_axis=0, tiled=True)  31.7 us
    all_to_all x1, starting transfers between devices, per_device(): whole = lax.all_to_all(v_li, 'ctx', split_axis=0, concat_axis=1, tiled=True)  21.9 us
  transfers between devices with their start and end apart: 2, of which 0 were waited for; matrix products, arithmetic and copies ran while one was open for 66% of the time, Pallas kernels for 0%

commit v1 on v0

v1 whole, which is shorter than its diff:
```python
import functools

import jax
import jax.numpy as jnp
from jax import lax
from jax.experimental import pallas as pl
from jax.experimental.pallas import tpu as pltpu
from jax.sharding import PartitionSpec as P

MESH = pl.DeviceIdType.MESH
F32 = jnp.float32
BF16 = jnp.bfloat16

CHANS = 64
ROWS = 512
HALF = 256
TAPS = 128
MODES = 16
LANES = 128


def packed(block):
    block = block.astype(F32)
    return jnp.concatenate([block[:, :HALF], block[:, HALF:]], axis=0).T


def kernel(
    group,
    q_mr,
    k_mr,
    v_mr,
    taps,
    gain,
    q_li,
    k_li,
    rates,
    residues,
    skip,
    out,
    in5,
    taps_in,
    gain_in,
    rates_in,
    residues_in,
    skip_in,
    a_own,
    rim,
    xs,
    far,
    tap_rows,
    wide,
    rate_rows,
    weight_rows,
    lift,
    filt,
    decay8,
    tail8,
    mr,
    sums_own,
    sums,
    vs,
    inner,
    state_own,
    states_z,
    total_own,
    states_y,
    result,
    in_sem,
    rim_sem,
    sums_send,
    sums_recv,
    z_send,
    z_recv,
    y_send,
    y_recv,
    out_sem,
):
    n_ctx, n_ch = lax.axis_size("ctx"), lax.axis_size("ch")
    n_y = n_ctx // group
    ctx, ch = lax.axis_index("ctx"), lax.axis_index("ch")
    place, plane = lax.rem(ctx, group), lax.div(ctx, group)

    rim[...] = jnp.zeros_like(rim)
    states_y[...] = jnp.zeros_like(states_y)

    barrier = pltpu.get_barrier_semaphore()

    def greet(device):
        pl.semaphore_signal(barrier, inc=1, device_id=device, device_id_type=MESH)

    @pl.when(ctx > 0)
    def _():
        greet({"ctx": ctx - 1, "ch": ch})

    @pl.when(ctx < n_ctx - 1)
    def _():
        greet({"ctx": ctx + 1, "ch": ch})

    for k in range(1, n_ch):
        greet({"ctx": ctx, "ch": lax.rem(ch + k, n_ch)})
    for k in range(1, group):
        greet({"ctx": plane * group + lax.rem(place + k, group), "ch": ch})
    for k in range(1, n_y):
        greet({"ctx": lax.rem(plane + k, n_y) * group + place, "ch": ch})

    loads = [
        pltpu.make_async_copy(src, dst, in_sem.at[i])
        for i, (src, dst) in enumerate(
            [
                (k_mr, in5.at[0]),
                (v_mr, in5.at[1]),
                (taps, taps_in),
                (rates, rates_in),
                (residues, residues_in),
                (q_mr, in5.at[2]),
                (k_li, in5.at[3]),
                (q_li, in5.at[4]),
                (gain, gain_in),
                (skip, skip_in),
            ]
        )
    ]
    for load in loads:
        load.start()

    lane = lax.broadcasted_iota(jnp.int32, (1, LANES), 1)
    first_half = lane < CHANS

    loads[0].wait()
    loads[1].wait()
    a = (in5[0].astype(F32) * in5[1].astype(F32)).astype(BF16)
    a_own[...] = a[:, ROWS - TAPS :]
    a_t = packed(a)
    xs[TAPS:, :] = a_t
    xs[:TAPS, :] = jnp.where(first_half, 0.0, pltpu.roll(a_t[HALF - TAPS :], CHANS, 1))
    far[TAPS:, :] = jnp.zeros((CHANS, LANES), F32)

    for load in loads[2:]:
        load.wait()
    tap_half = taps_in[...].astype(F32)
    tap_rows[...] = jnp.concatenate([tap_half, tap_half], axis=0).T

    def doubled(ref):
        wide[...] = jnp.zeros_like(wide)
        wide[:, :CHANS] = ref[...]
        return wide[...] + pltpu.roll(wide[...], CHANS, 1)

    rate = doubled(rates_in)
    weight = doubled(residues_in) * jnp.sqrt(rate)
    rate_rows[...] = rate
    weight_rows[...] = weight

    def doubled_row(ref):
        wide[...] = jnp.zeros_like(wide)
        wide[:1, :CHANS] = ref[...]
        return (wide[...] + pltpu.roll(wide[...], CHANS, 1))[:1]

    gain_row = doubled_row(gain_in)
    skip_row = doubled_row(skip_in)

    ends = jnp.where(ctx > 0, 1, 0) + jnp.where(ctx < n_ctx - 1, 1, 0)
    pl.semaphore_wait(barrier, n_ch - 1 + group - 1 + n_y - 1 + ends)

    def send_rim():
        return pltpu.make_async_remote_copy(
            src_ref=a_own,
            dst_ref=rim,
            send_sem=rim_sem.at[0],
            recv_sem=rim_sem.at[1],
            device_id={"ctx": ctx + 1, "ch": ch},
            device_id_type=MESH,
        )

    @pl.when(ctx < n_ctx - 1)
    def _():
        send_rim().start()

    def tap_step(i, acc):
        base = TAPS - 8 * i
        for p in range(8):
            acc = acc + xs[pl.ds(base - p, HALF), :] * tap_rows[pl.ds(8 * i + p, 1), :]
        return acc

    mr[...] = lax.fori_loop(0, TAPS // 8, tap_step, jnp.zeros((HALF, LANES), F32))

    times = lax.broadcasted_iota(jnp.int32, (HALF, LANES), 0).astype(F32)
    filt[...] = jnp.zeros_like(filt)

    @pl.loop(0, MODES)
    def _(r):
        term = jnp.exp(-rate_rows[pl.ds(r, 1), :] * times) * weight_rows[pl.ds(r, 1), :]
        lift[r] = term
        filt[...] += term

    offset8 = lax.broadcasted_iota(jnp.int32, (1, 8, LANES), 1).astype(F32)
    decay8[...] = jnp.broadcast_to(jnp.exp(rate * -8.0)[:, None, :], (MODES, 8, LANES))
    tail8[...] = jnp.exp(-rate[:, None, :] * (7.0 - offset8))

    q_t = packed(in5[2])
    k_t = packed(in5[3])

    @pl.when(ctx > 0)
    def _():
        send_rim().wait_recv()

    rim_now = rim[...].astype(F32)
    later = jnp.where(first_half, pltpu.roll(rim_now, CHANS, 1), 0.0)
    far[:TAPS, :] = jnp.concatenate([rim_now, later], axis=0).T

    def far_step(i, acc):
        base = TAPS - 8 * i
        for p in range(8):
            acc = acc + far[pl.ds(base - p, CHANS), :] * tap_rows[pl.ds(8 * i + p, 1), :]
        return acc

    reach = lax.fori_loop(0, TAPS // 8, far_step, jnp.zeros((CHANS, LANES), F32))
    mr[:CHANS, :] += jnp.where(first_half, reach, 0.0)
    mr[CHANS:TAPS, :] += jnp.where(first_half, pltpu.roll(reach, CHANS, 1), 0.0)

    gated = q_t * mr[...]
    squares = (gated * gated).T
    mine = jnp.concatenate(
        [
            jnp.sum(squares[:CHANS], axis=0, keepdims=True),
            jnp.sum(squares[CHANS:], axis=0, keepdims=True),
        ],
        axis=0,
    )
    sums_own[...] = mine
    sums[ch] = mine

    def send_sums(peer, slot):
        return pltpu.make_async_remote_copy(
            src_ref=sums_own,
            dst_ref=sums.at[slot],
            send_sem=sums_send.at[peer],
            recv_sem=sums_recv.at[slot],
            device_id={"ctx": ctx, "ch": peer},
            device_id_type=MESH,
        )

    for k in range(1, n_ch):
        send_sums(lax.rem(ch + k, n_ch), ch).start()
    raised = k_t * gated
    for k in range(1, n_ch):
        peer = lax.rem(ch + k, n_ch)
        send_sums(peer, peer).wait_recv()

    total = sums[0]
    for k in range(1, n_ch):
        total = total + sums[k]
    inv = lax.rsqrt(total / (n_ch * CHANS) + 1e-05)
    inv_t = jnp.concatenate(
        [
            jnp.broadcast_to(inv[:1], (CHANS, HALF)),
            jnp.broadcast_to(inv[1:], (CHANS, HALF)),
        ],
        axis=0,
    ).T
    v = (raised * inv_t * gain_row).astype(BF16).astype(F32)
    vs[:HALF, :] = jnp.zeros((HALF, LANES), F32)
    vs[HALF:, :] = v

    keep = decay8[...]
    acc = jnp.broadcast_to(v[None, :8], (MODES, 8, LANES))
    for i in range(1, HALF // 8):
        acc = acc * keep + v[None, 8 * i : 8 * i + 8]
    ends_half = jnp.sum(acc * tail8[...], axis=1)
    decay_half = jnp.exp(rate * -float(HALF))
    aged = jnp.where(first_half, ends_half * decay_half, ends_half)
    state = aged + pltpu.roll(aged, CHANS, 1)
    from_first = pltpu.roll(ends_half, CHANS, 1)

    def folded(x):
        return jnp.where(first_half, x[:8], x[8:])

    state_own[...] = folded(state)
    states_z[place] = folded(state)

    def send_z(peer, slot):
        return pltpu.make_async_remote_copy(
            src_ref=state_own,
            dst_ref=states_z.at[slot],
            send_sem=z_send.at[peer],
            recv_sem=z_recv.at[slot],
            device_id={"ctx": plane * group + peer, "ch": ch},
            device_id_type=MESH,
        )

    for k in range(1, group):
        send_z(lax.rem(place + k, group), place).start()

    inner[...] = skip_row * v
    block = 64
    for b in range(HALF // block):
        low = b * block

        def filt_step(i, acc, low=low):
            base = HALF - 8 * i
            for p in range(8):
                acc = acc + vs[pl.ds(base - p, HALF - low), :] * filt[pl.ds(low + 8 * i + p, 1), :]
            return acc

        inner[low:, :] += lax.fori_loop(
            0, block // 8, filt_step, jnp.zeros((HALF - low, LANES), F32)
        )
    ql_t = packed(in5[4])
    rate_folded = folded(rate)
    decay_one = jnp.exp(rate_folded * -float(ROWS))
    decay_plane = jnp.exp(rate_folded * -float(ROWS * group))
    decay_place = jnp.exp(rate_folded * (place.astype(F32) * -float(ROWS)))

    for k in range(1, group):
        peer = lax.rem(place + k, group)
        send_z(peer, peer).wait_recv()
    run = jnp.zeros((8, LANES), F32)
    before = jnp.zeros((8, LANES), F32)
    for k in range(group):
        before = jnp.where(place == k, run, before)
        run = run * decay_one + states_z[k]
    total_own[...] = run

    def send_y(peer, slot):
        return pltpu.make_async_remote_copy(
            src_ref=total_own,
            dst_ref=states_y.at[slot],
            send_sem=y_send.at[peer],
            recv_sem=y_recv.at[slot],
            device_id={"ctx": peer * group + place, "ch": ch},
            device_id_type=MESH,
        )

    for k in range(1, n_y):

        @pl.when(plane + k < n_y)
        def _(k=k):
            send_y(plane + k, plane).start()

    for k in range(1, n_y):

        @pl.when(plane - k >= 0)
        def _(k=k):
            send_y(plane - k, plane - k).wait_recv()

    carry = jnp.zeros((8, LANES), F32)
    for k in range(n_y - 1):
        carry = jnp.where(plane > k, carry * decay_plane + states_y[k], carry)
    carry = before + decay_place * carry

    low = jnp.where(first_half, carry, 0.0)
    high = jnp.where(first_half, 0.0, carry)
    carry = jnp.concatenate(
        [low + pltpu.roll(low, CHANS, 1), high + pltpu.roll(high, CHANS, 1)], axis=0
    )
    carry = jnp.where(first_half, carry, carry * decay_half + from_first)
    carry = carry * jnp.exp(-rate)
    acc = inner[...]
    for r in range(MODES):
        acc = acc + lift[r] * carry[r : r + 1]
    mixed = (ql_t * acc.astype(BF16).astype(F32)).T.astype(BF16)
    result[:, :HALF] = mixed[:CHANS]
    result[:, HALF:] = mixed[CHANS:]
    store = pltpu.make_async_copy(result, out, out_sem)
    store.start()

    @pl.when(ctx < n_ctx - 1)
    def _():
        send_rim().wait_send()

    for k in range(1, n_ch):
        send_sums(lax.rem(ch + k, n_ch), ch).wait_send()
    for k in range(1, group):
        send_z(lax.rem(place + k, group), place).wait_send()
    for k in range(1, n_y):

        @pl.when(plane + k < n_y)
        def _(k=k):
            send_y(plane + k, plane).wait_send()

    store.wait()


def build(mesh, group):
    n_ctx, n_ch = mesh.shape["ctx"], mesh.shape["ch"]
    n_y = n_ctx // group

    def per_device(q_mr, k_mr, v_mr, taps, gain, q_li, k_li, rates, residues, skip):
        dma = pltpu.SemaphoreType.DMA
        any_spec = pl.BlockSpec(memory_space=pl.ANY)
        return pl.pallas_call(
            functools.partial(kernel, group),
            out_shape=jax.ShapeDtypeStruct((CHANS, ROWS), BF16),
            in_specs=[any_spec] * 10,
            out_specs=any_spec,
            scratch_shapes=[
                pltpu.VMEM((5, CHANS, ROWS), BF16),
                pltpu.VMEM((CHANS, TAPS), BF16),
                pltpu.VMEM((1, CHANS), F32),
                pltpu.VMEM((MODES, CHANS), F32),
                pltpu.VMEM((MODES, CHANS), F32),
                pltpu.VMEM((1, CHANS), F32),
                pltpu.VMEM((CHANS, TAPS), BF16),
                pltpu.VMEM((CHANS, TAPS), BF16),
                pltpu.VMEM((TAPS + HALF, LANES), F32),
                pltpu.VMEM((TAPS + CHANS, LANES), F32),
                pltpu.VMEM((TAPS, LANES), F32),
                pltpu.VMEM((MODES, LANES), F32),
                pltpu.VMEM((MODES, LANES), F32),
                pltpu.VMEM((MODES, LANES), F32),
                pltpu.VMEM((MODES, HALF, LANES), F32),
                pltpu.VMEM((HALF, LANES), F32),
                pltpu.VMEM((MODES, 8, LANES), F32),
                pltpu.VMEM((MODES, 8, LANES), F32),
                pltpu.VMEM((HALF, LANES), F32),
                pltpu.VMEM((2, HALF), F32),
                pltpu.VMEM((n_ch, 2, HALF), F32),
                pltpu.VMEM((2 * HALF, LANES), F32),
                pltpu.VMEM((HALF, LANES), F32),
                pltpu.VMEM((8, LANES), F32),
                pltpu.VMEM((group, 8, LANES), F32),
                pltpu.VMEM((8, LANES), F32),
                pltpu.VMEM((n_y, 8, LANES), F32),
                pltpu.VMEM((CHANS, ROWS), BF16),
                dma((10,)),
                dma((2,)),
                dma((n_ch,)),
                dma((n_ch,)),
                dma((group,)),
                dma((group,)),
                dma((n_y,)),
                dma((n_y,)),
                dma,
            ],
            compiler_params=pltpu.CompilerParams(collective_id=0, has_side_effects=True),
            name="hyena_pair",
        )(
            q_mr,
            k_mr,
            v_mr,
            taps.T,
            gain.reshape(1, CHANS),
            q_li,
            k_li,
            rates.T,
            residues.T,
            skip.reshape(1, CHANS),
        )

    placed = (
        P("ch", "ctx"),
        P("ch", "ctx"),
        P("ch", "ctx"),
        P(None, "ch"),
        P("ch"),
        P("ch", "ctx"),
        P("ch", "ctx"),
        P("ch", None),
        P("ch", None),
        P("ch"),
    )
    return jax.shard_map(
        per_device, mesh=mesh, in_specs=placed, out_specs=P("ch", "ctx"), check_vma=False
    )


def solution(mesh):
    return build(mesh, 8)
```

time: 349 us -> 47.7 us (0.14); the launches traced: 344 us -> 47.5 us
  local copies, waits for them, and re-layouts: 231 us -> 1.47 us
  blocking collectives: 77.7 us -> 0 us
  Pallas kernels: 0 us -> 46 us
  starting transfers between devices: 23.8 us -> 0 us
  other arithmetic: 7.12 us -> 0 us
  matrix products: 4.34 us -> 0 us
    gather x5 -> x0, local copies, waits for them, and re-layouts: 222 us -> none  [banded(): table = column[:, jnp.clip(lag, 0, width - 1)]]
    pallas_call x0 -> x1, Pallas kernels: none -> 46 us  [per_device(): pl.pallas_call(functools.partial(kernel, group), out_shape=jax.ShapeDtype...]
    psum x1 -> x0, blocking collectives: 46 us -> none  [per_device(): total = lax.psum(jnp.sum(gated * gated, axis=0), 'ch')]
    all_to_all x1 -> x0, blocking collectives: 31.7 us -> none  [per_device(): lax.all_to_all(owned, 'ctx', split_axis=1, concat_axis=0, tiled=True)]
    all_to_all x1 -> x0, starting transfers between devices: 21.9 us -> none  [per_device(): whole = lax.all_to_all(v_li, 'ctx', split_axis=0, concat_axis=1, tiled=True)]
    dot_general x6 -> x0, matrix products: 4.34 us -> none  [the longest x1 1.18 us: per_device(): jnp.einsum('cij,cnj->cni', near, blocks, preferred_element_type=jnp.float32)]
  transfers between devices with their start and end apart: 2 -> 0, of which waited for: 0 -> 0; matrix products, arithmetic and copies ran while one was open for 66% -> 0% of each run, Pallas kernels for 0% -> 0%
where the time goes in v1:
time: 47.7 us; the launch traced here: 47.5 us
  Pallas kernels  46 us (96%)
  local copies, waits for them, and re-layouts  1.47 us (3%)
    pallas_call x1, Pallas kernels, per_device(): pl.pallas_call(functools.partial(kernel, group), out_shape=jax.ShapeDtype...  46 us
    unnamed x1, local copies, waits for them, and re-layouts  1.47 us

profile of v1, /device:TPU:56, one launch (start us, length us, event | category | flops | bytes accessed | tf_op | source)
XLA Modules:
  0.0 47.5 jit_solution(17337204386701590662)
XLA Ops:
  0.0 46.0 %hyena_pair.1 = bf16[64,512]{1,0:T(8,128)(2,1)} custom-call(bf16[64,512]{1,0:T(8,128)(2,1)} %q_mr.1, bf16[64,512]{1,0:T(8,128)(2,1)} %k_mr.1, bf16[64,512]{1,0:T(8,128)(2,1)} %v_mr.1, bf16[64,128]{1,0:T(8,128)(2,1)} %bitcast.5, f32[1,64]{1,0:T(1,128)} %bitcast.8, bf16[64,512]{1,0:T(8,128)(2,1)} %q_li.1, bf16[64,512]{1,0:T(8,128)(2,1)} %k_li.1, ...), custom_call_target="tpu_custom_call" | custom-call | tf_op jit(solution)/shard_map/hyena_pair/pallas_call | solution.py:390
  46.0 1.5 %copy.12 = bf16[64,512]{1,0:T(8,128)(2,1)} copy(bf16[64,512]{1,0:T(8,128)(2,1)} %hyena_pair.1) | data formatting | bytes 131072

commit v2 on v1

--- a/solution.py
+++ b/solution.py
@@ -43,6 +43,7 @@
     rates_in,
     residues_in,
     skip_in,
+    tails,
     a_own,
     rim,
     xs,
@@ -74,11 +75,79 @@
     y_send,
     y_recv,
     out_sem,
+    far_ready,
+    first_ready,
+    ends_ready,
+    early_own,
+    early,
+    first_own,
+    first,
+    raised_own,
+    raised_in,
+    main_own,
+    main_in,
+    early_send,
+    early_recv,
+    first_send,
+    first_recv,
+    raised_sem,
+    main_sem,
 ):
     n_ctx, n_ch = lax.axis_size("ctx"), lax.axis_size("ch")
     n_y = n_ctx // group
     ctx, ch = lax.axis_index("ctx"), lax.axis_index("ch")
     place, plane = lax.rem(ctx, group), lax.div(ctx, group)
+    core = lax.rem(ctx, 2)
+    n_z = group // 2
+    z = lax.div(place, 2)
+
+    def at(dz, dcore):
+        return 2 * lax.rem(z + dz, n_z) + lax.rem(core + dcore, 2)
+
+    others = [(dz, dc) for dz in range(n_z) for dc in (0, 1) if (dz, dc) != (0, 0)]
+    others = others[1:] + others[:1]
+
+    hasty = (z == 2) & (core == 0) if n_z == 4 else None
+
+    def column_sums(gated):
+        squares = (gated * gated).T
+        return jnp.concatenate(
+            [
+                jnp.sum(squares[:CHANS], axis=0, keepdims=True),
+                jnp.sum(squares[CHANS:], axis=0, keepdims=True),
+            ],
+            axis=0,
+        )
+
+    def send_early(peer, slot):
+        return pltpu.make_async_remote_copy(
+            src_ref=early_own,
+            dst_ref=early.at[slot],
+            send_sem=early_send.at[peer],
+            recv_sem=early_recv.at[slot],
+            device_id={"ctx": ctx, "ch": peer},
+            device_id_type=MESH,
+        )
+
+    def send_first(dcore, peer, slot):
+        return pltpu.make_async_remote_copy(
+            src_ref=first_own,
+            dst_ref=first.at[slot],
+            send_sem=first_send.at[dcore * n_ch + peer],
+            recv_sem=first_recv.at[slot],
+            device_id={"ctx": plane * group + dcore, "ch": peer},
+            device_id_type=MESH,
+        )
+
+    def send_plain(src, dst, sem, dcore):
+        return pltpu.make_async_remote_copy(
+            src_ref=src,
+            dst_ref=dst,
+            send_sem=sem.at[dcore],
+            recv_sem=sem.at[2],
+            device_id={"ctx": plane * group + dcore, "ch": ch},
+            device_id_type=MESH,
+        )
 
     rim[...] = jnp.zeros_like(rim)
     states_y[...] = jnp.zeros_like(states_y)
@@ -88,25 +157,36 @@
     def greet(device):
         pl.semaphore_signal(barrier, inc=1, device_id=device, device_id_type=MESH)
 
-    @pl.when(ctx > 0)
+    def in_group(dz, dcore):
+        return {"ctx": plane * group + at(dz, dcore), "ch": ch}
+
+    @pl.when((place == 0) & (plane > 0))
     def _():
         greet({"ctx": ctx - 1, "ch": ch})
 
-    @pl.when(ctx < n_ctx - 1)
+    @pl.when(z > 0)
     def _():
-        greet({"ctx": ctx + 1, "ch": ch})
-
+        for dc in (1, 0):
+            greet(in_group(n_z - 1, dc))
+
+    @pl.when(z < n_z - 1)
+    def _():
+        for dc in (0, 1):
+            greet(in_group(1, dc))
+
+    greet(in_group(0, 1))
     for k in range(1, n_ch):
         greet({"ctx": ctx, "ch": lax.rem(ch + k, n_ch)})
-    for k in range(1, group):
-        greet({"ctx": plane * group + lax.rem(place + k, group), "ch": ch})
     for k in range(1, n_y):
         greet({"ctx": lax.rem(plane + k, n_y) * group + place, "ch": ch})
 
+    tail = pl.ds(ROWS - TAPS, TAPS)
     loads = [
         pltpu.make_async_copy(src, dst, in_sem.at[i])
         for i, (src, dst) in enumerate(
             [
+                (k_mr.at[:, tail], tails.at[0]),
+                (v_mr.at[:, tail], tails.at[1]),
                 (k_mr, in5.at[0]),
                 (v_mr, in5.at[1]),
                 (taps, taps_in),
@@ -128,14 +208,16 @@
 
     loads[0].wait()
     loads[1].wait()
+    a_own[...] = (tails[0].astype(F32) * tails[1].astype(F32)).astype(BF16)
+    loads[2].wait()
+    loads[3].wait()
     a = (in5[0].astype(F32) * in5[1].astype(F32)).astype(BF16)
-    a_own[...] = a[:, ROWS - TAPS :]
     a_t = packed(a)
     xs[TAPS:, :] = a_t
     xs[:TAPS, :] = jnp.where(first_half, 0.0, pltpu.roll(a_t[HALF - TAPS :], CHANS, 1))
     far[TAPS:, :] = jnp.zeros((CHANS, LANES), F32)
 
-    for load in loads[2:]:
+    for load in loads[4:]:
         load.wait()
     tap_half = taps_in[...].astype(F32)
     tap_rows[...] = jnp.concatenate([tap_half, tap_half], axis=0).T
@@ -158,8 +240,25 @@
     gain_row = doubled_row(gain_in)
     skip_row = doubled_row(skip_in)
 
-    ends = jnp.where(ctx > 0, 1, 0) + jnp.where(ctx < n_ctx - 1, 1, 0)
-    pl.semaphore_wait(barrier, n_ch - 1 + group - 1 + n_y - 1 + ends)
+    q_t = packed(in5[2])
+    k_t = packed(in5[3])
+
+    def tap_step(i, acc):
+        base = TAPS - 8 * i
+        for p in range(8):
+            acc = acc + xs[pl.ds(base - p, HALF), :] * tap_rows[pl.ds(8 * i + p, 1), :]
+        return acc
+
+    def own_taps():
+        mr[...] = lax.fori_loop(0, TAPS // 8, tap_step, jnp.zeros((HALF, LANES), F32))
+
+    if n_z == 4:
+        pl.when(hasty)(own_taps)
+
+    greeted = n_ch - 1 + n_y - 1 + 1
+    greeted += jnp.where(z > 0, 2, 0) + jnp.where(z < n_z - 1, 2, 0)
+    greeted += jnp.where((place == group - 1) & (plane < n_y - 1), 1, 0)
+    pl.semaphore_wait(barrier, greeted)
 
     def send_rim():
         return pltpu.make_async_remote_copy(
@@ -175,29 +274,38 @@
     def _():
         send_rim().start()
 
-    def tap_step(i, acc):
-        base = TAPS - 8 * i
-        for p in range(8):
-            acc = acc + xs[pl.ds(base - p, HALF), :] * tap_rows[pl.ds(8 * i + p, 1), :]
-        return acc
-
-    mr[...] = lax.fori_loop(0, TAPS // 8, tap_step, jnp.zeros((HALF, LANES), F32))
-
-    times = lax.broadcasted_iota(jnp.int32, (HALF, LANES), 0).astype(F32)
-    filt[...] = jnp.zeros_like(filt)
-
-    @pl.loop(0, MODES)
-    def _(r):
-        term = jnp.exp(-rate_rows[pl.ds(r, 1), :] * times) * weight_rows[pl.ds(r, 1), :]
-        lift[r] = term
-        filt[...] += term
-
-    offset8 = lax.broadcasted_iota(jnp.int32, (1, 8, LANES), 1).astype(F32)
-    decay8[...] = jnp.broadcast_to(jnp.exp(rate * -8.0)[:, None, :], (MODES, 8, LANES))
-    tail8[...] = jnp.exp(-rate[:, None, :] * (7.0 - offset8))
-
-    q_t = packed(in5[2])
-    k_t = packed(in5[3])
+    def tell(sem, dz, dcore):
+        pl.semaphore_signal(sem, inc=1, device_id=in_group(dz, dcore), device_id_type=MESH)
+
+    if n_z == 4:
+
+        @pl.when(z == 0)
+        def _():
+            tell(first_ready, 1, 0)
+
+        @pl.when(z == 1)
+        def _():
+            pl.semaphore_wait(first_ready, 1)
+            tell(far_ready, 1, 0)
+            tell(ends_ready, 1, core)
+
+        @pl.when(z == 2)
+        def _():
+            tell(far_ready, n_z - 1, 0)
+
+        @pl.when(hasty)
+        def _():
+            gated = q_t * mr[...]
+            mine = column_sums(gated)
+            early_own[...] = mine
+            early[ch] = mine
+            for k in range(1, n_ch):
+                send_early(lax.rem(ch + k, n_ch), ch).start()
+
+    if n_z == 4:
+        pl.when(jnp.logical_not(hasty))(own_taps)
+    else:
+        own_taps()
 
     @pl.when(ctx > 0)
     def _():
@@ -218,14 +326,7 @@
     mr[CHANS:TAPS, :] += jnp.where(first_half, pltpu.roll(reach, CHANS, 1), 0.0)
 
     gated = q_t * mr[...]
-    squares = (gated * gated).T
-    mine = jnp.concatenate(
-        [
-            jnp.sum(squares[:CHANS], axis=0, keepdims=True),
-            jnp.sum(squares[CHANS:], axis=0, keepdims=True),
-        ],
-        axis=0,
-    )
+    mine = column_sums(gated)
     sums_own[...] = mine
     sums[ch] = mine
 
@@ -242,40 +343,103 @@
     for k in range(1, n_ch):
         send_sums(lax.rem(ch + k, n_ch), ch).start()
     raised = k_t * gated
+
+    if n_z == 4:
+
+        @pl.when(hasty)
+        def _():
+            pl.semaphore_wait(ends_ready, 2)
+            first_own[...] = mine[:1, :TAPS]
+            for dcore in (0, 1):
+                for k in range(n_ch):
+                    send_first(dcore, lax.rem(ch + k, n_ch), ch).start()
+            raised_own[...] = jnp.where(
+                first_half, raised[:CHANS], pltpu.roll(raised[CHANS:TAPS], CHANS, 1)
+            ).astype(BF16)
+            for dcore in (0, 1):
+                send_plain(raised_own, raised_in, raised_sem, dcore).start()
+
+    if n_z == 4:
+
+        @pl.when(z == 1)
+        def _():
+            pl.semaphore_wait(far_ready, 1)
+            tell(far_ready, n_z - 1, 0)
+
+        @pl.when(z == 2)
+        def _():
+            pl.semaphore_wait(far_ready, 1)
+            tell(far_ready, 1, 0)
+
+    times = lax.broadcasted_iota(jnp.int32, (HALF, LANES), 0).astype(F32)
+    filt[...] = jnp.zeros_like(filt)
+
+    @pl.loop(0, MODES)
+    def _(r):
+        term = jnp.exp(-rate_rows[pl.ds(r, 1), :] * times) * weight_rows[pl.ds(r, 1), :]
+        lift[r] = term
+        filt[...] += term
+
+    offset8 = lax.broadcasted_iota(jnp.int32, (1, 8, LANES), 1).astype(F32)
+    decay8[...] = jnp.broadcast_to(jnp.exp(rate * -8.0)[:, None, :], (MODES, 8, LANES))
+    tail8[...] = jnp.exp(-rate[:, None, :] * (7.0 - offset8))
+
+    def normed(sums):
+        total = sums[0]
+        for k in range(1, n_ch):
+            total = total + sums[k]
+        inv = lax.rsqrt(total / (n_ch * CHANS) + 1e-05)
+        inv_t = jnp.concatenate(
+            [
+                jnp.broadcast_to(inv[:1], (CHANS, HALF)),
+                jnp.broadcast_to(inv[1:], (CHANS, HALF)),
+            ],
+            axis=0,
+        ).T
+        return (raised * inv_t * gain_row).astype(BF16).astype(F32)
+
+    def ends_of(v):
+        keep = decay8[...]
+        acc = jnp.broadcast_to(v[None, :8], (MODES, 8, LANES))
+        for i in range(1, v.shape[0] // 8):
+            acc = acc * keep + v[None, 8 * i : 8 * i + 8]
+        return jnp.sum(acc * tail8[...], axis=1)
+
+    def folded(x):
+        return jnp.where(first_half, x[:8], x[8:])
+
+    def joined(aged):
+        return folded(aged + pltpu.roll(aged, CHANS, 1))
+
+    decay_half = jnp.exp(rate * -float(HALF))
+
+    if n_z == 4:
+
+        @pl.when(hasty)
+        def _():
+            for k in range(1, n_ch):
+                peer = lax.rem(ch + k, n_ch)
+                send_early(peer, peer).wait_recv()
+            row = lax.broadcasted_iota(jnp.int32, (HALF, LANES), 0)
+            v = jnp.where(first_half & (row < TAPS), 0.0, normed(early))
+            ends = ends_of(v)
+            main_own[...] = joined(jnp.where(first_half, ends * decay_half, ends))
+            for dcore in (0, 1):
+                send_plain(main_own, main_in, main_sem, dcore).start()
+
     for k in range(1, n_ch):
         peer = lax.rem(ch + k, n_ch)
         send_sums(peer, peer).wait_recv()
 
-    total = sums[0]
-    for k in range(1, n_ch):
-        total = total + sums[k]
-    inv = lax.rsqrt(total / (n_ch * CHANS) + 1e-05)
-    inv_t = jnp.concatenate(
-        [
-            jnp.broadcast_to(inv[:1], (CHANS, HALF)),
-            jnp.broadcast_to(inv[1:], (CHANS, HALF)),
-        ],
-        axis=0,
-    ).T
-    v = (raised * inv_t * gain_row).astype(BF16).astype(F32)
+    v = normed(sums)
     vs[:HALF, :] = jnp.zeros((HALF, LANES), F32)
     vs[HALF:, :] = v
 
-    keep = decay8[...]
-    acc = jnp.broadcast_to(v[None, :8], (MODES, 8, LANES))
-    for i in range(1, HALF // 8):
-        acc = acc * keep + v[None, 8 * i : 8 * i + 8]
-    ends_half = jnp.sum(acc * tail8[...], axis=1)
-    decay_half = jnp.exp(rate * -float(HALF))
-    aged = jnp.where(first_half, ends_half * decay_half, ends_half)
-    state = aged + pltpu.roll(aged, CHANS, 1)
+    ends_half = ends_of(v)
+    state = joined(jnp.where(first_half, ends_half * decay_half, ends_half))
     from_first = pltpu.roll(ends_half, CHANS, 1)
-
-    def folded(x):
-        return jnp.where(first_half, x[:8], x[8:])
-
-    state_own[...] = folded(state)
-    states_z[place] = folded(state)
+    state_own[...] = state
+    states_z[place] = state
 
     def send_z(peer, slot):
         return pltpu.make_async_remote_copy(
@@ -287,8 +451,26 @@
             device_id_type=MESH,
         )
 
-    for k in range(1, group):
-        send_z(lax.rem(place + k, group), place).start()
+    if n_z == 4:
+
+        @pl.when((z == 0) | (z == n_z - 1))
+        def _():
+            pl.semaphore_wait(far_ready, 1)
+
+    def for_others(act, sending):
+        for step in others:
+            peer = at(*step)
+            if n_z == 4 and step[0] == 2:
+                skip_it = hasty if sending else (z == 0) & (lax.rem(peer, 2) == 0)
+
+                @pl.when(jnp.logical_not(skip_it))
+                def _(peer=peer):
+                    act(send_z(peer, place if sending else peer))
+
+            else:
+                act(send_z(peer, place if sending else peer))
+
+    for_others(lambda copy: copy.start(), True)
 
     inner[...] = skip_row * v
     block = 64
@@ -310,9 +492,31 @@
     decay_plane = jnp.exp(rate_folded * -float(ROWS * group))
     decay_place = jnp.exp(rate_folded * (place.astype(F32) * -float(ROWS)))
 
-    for k in range(1, group):
-        peer = lax.rem(place + k, group)
-        send_z(peer, peer).wait_recv()
+    if n_z == 4:
+
+        @pl.when(z == 0)
+        def _():
+            for k in range(n_ch):
+                send_first(0, k, k).wait_recv()
+            total = first[0]
+            for k in range(1, n_ch):
+                total = total + first[k]
+            inv = lax.rsqrt(total / (n_ch * CHANS) + 1e-05)
+            inv_t = jnp.concatenate(
+                [
+                    jnp.broadcast_to(inv, (CHANS, LANES)),
+                    jnp.broadcast_to(pltpu.roll(inv, CHANS, 1), (CHANS, LANES)),
+                ],
+                axis=0,
+            ).T[:CHANS]
+            send_plain(raised_own, raised_in, raised_sem, 0).wait_recv()
+            v = (raised_in[...].astype(F32) * inv_t * gain_row).astype(BF16).astype(F32)
+            age = jnp.where(first_half, float(ROWS - CHANS), float(ROWS - TAPS))
+            added = joined(ends_of(v) * jnp.exp(-rate * age))
+            send_plain(main_own, main_in, main_sem, 0).wait_recv()
+            states_z[4] = main_in[...] + added
+
+    for_others(lambda copy: copy.wait_recv(), False)
     run = jnp.zeros((8, LANES), F32)
     before = jnp.zeros((8, LANES), F32)
     for k in range(group):
@@ -360,8 +564,7 @@
     mixed = (ql_t * acc.astype(BF16).astype(F32)).T.astype(BF16)
     result[:, :HALF] = mixed[:CHANS]
     result[:, HALF:] = mixed[CHANS:]
-    store = pltpu.make_async_copy(result, out, out_sem)
-    store.start()
+    out[...] = result[...]
 
     @pl.when(ctx < n_ctx - 1)
     def _():
@@ -369,15 +572,24 @@
 
     for k in range(1, n_ch):
         send_sums(lax.rem(ch + k, n_ch), ch).wait_send()
-    for k in range(1, group):
-        send_z(lax.rem(place + k, group), place).wait_send()
+    for_others(lambda copy: copy.wait_send(), True)
+    if n_z == 4:
+
+        @pl.when(hasty)
+        def _():
+            for k in range(1, n_ch):
+                send_early(lax.rem(ch + k, n_ch), ch).wait_send()
+            for dcore in (0, 1):
+                for k in range(n_ch):
+                    send_first(dcore, lax.rem(ch + k, n_ch), ch).wait_send()
+                send_plain(raised_own, raised_in, raised_sem, dcore).wait_send()
+                send_plain(main_own, main_in, main_sem, dcore).wait_send()
+
     for k in range(1, n_y):
 
         @pl.when(plane + k < n_y)
         def _(k=k):
             send_y(plane + k, plane).wait_send()
-
-    store.wait()
 
 
 def build(mesh, group):
@@ -389,9 +601,9 @@
         any_spec = pl.BlockSpec(memory_space=pl.ANY)
         return pl.pallas_call(
             functools.partial(kernel, group),
-            out_shape=jax.ShapeDtypeStruct((CHANS, ROWS), BF16),
+            out_shape=pltpu.VMEM((CHANS, ROWS), BF16),
             in_specs=[any_spec] * 10,
-            out_specs=any_spec,
+            out_specs=pl.BlockSpec(memory_space=pltpu.VMEM),
             scratch_shapes=[
                 pltpu.VMEM((5, CHANS, ROWS), BF16),
                 pltpu.VMEM((CHANS, TAPS), BF16),
@@ -399,6 +611,7 @@
                 pltpu.VMEM((MODES, CHANS), F32),
                 pltpu.VMEM((MODES, CHANS), F32),
                 pltpu.VMEM((1, CHANS), F32),
+                pltpu.VMEM((2, CHANS, TAPS), BF16),
                 pltpu.VMEM((CHANS, TAPS), BF16),
                 pltpu.VMEM((CHANS, TAPS), BF16),
                 pltpu.VMEM((TAPS + HALF, LANES), F32),
@@ -421,7 +634,7 @@
                 pltpu.VMEM((8, LANES), F32),
                 pltpu.VMEM((n_y, 8, LANES), F32),
                 pltpu.VMEM((CHANS, ROWS), BF16),
-                dma((10,)),
+                dma((12,)),
                 dma((2,)),
                 dma((n_ch,)),
                 dma((n_ch,)),
@@ -430,6 +643,23 @@
                 dma((n_y,)),
                 dma((n_y,)),
                 dma,
+                pltpu.SemaphoreType.REGULAR,
+                pltpu.SemaphoreType.REGULAR,
+                pltpu.SemaphoreType.REGULAR,
+                pltpu.VMEM((2, HALF), F32),
+                pltpu.VMEM((n_ch, 2, HALF), F32),
+                pltpu.VMEM((1, TAPS), F32),
+                pltpu.VMEM((n_ch, 1, TAPS), F32),
+                pltpu.VMEM((CHANS, LANES), BF16),
+                pltpu.VMEM((CHANS, LANES), BF16),
+                pltpu.VMEM((8, LANES), F32),
+                pltpu.VMEM((8, LANES), F32),
+                dma((n_ch,)),
+                dma((n_ch,)),
+                dma((2 * n_ch,)),
+                dma((n_ch,)),
+                dma((3,)),
+                dma((3,)),
             ],
             compiler_params=pltpu.CompilerParams(collective_id=0, has_side_effects=True),
             name="hyena_pair",

time: 47.7 us -> 42 us (0.88)
  Pallas kernels: 46 us -> 41.2 us
  local copies, waits for them, and re-layouts: 1.47 us -> 0.63 us
    pallas_call x1, Pallas kernels: 46 us -> 41.2 us  [per_device(): pl.pallas_call(functools.partial(kernel, group), out_shape=pltpu.VMEM((CH...]
    unnamed x1, local copies, waits for them, and re-layouts: 1.47 us -> 0.63 us
where the time goes in v2:
time: 42 us; the launch traced here: 41.8 us
  Pallas kernels  41.2 us (98%)
  local copies, waits for them, and re-layouts  0.63 us (2%)
    pallas_call x1, Pallas kernels, per_device(): pl.pallas_call(functools.partial(kernel, group), out_shape=pltpu.VMEM((CH...  41.2 us

profile of v2, /device:TPU:56, one launch (start us, length us, event | category | flops | bytes accessed | tf_op | source)
XLA Modules:
  0.0 41.8 jit_solution(5585755286802190604)
XLA Ops:
  0.0 41.2 %hyena_pair.1 = bf16[64,512]{1,0:T(8,128)(2,1)S(1)} custom-call(bf16[64,512]{1,0:T(8,128)(2,1)} %q_mr.1, bf16[64,512]{1,0:T(8,128)(2,1)} %k_mr.1, bf16[64,512]{1,0:T(8,128)(2,1)} %v_mr.1, bf16[64,128]{1,0:T(8,128)(2,1)} %bitcast.5, f32[1,64]{1,0:T(1,128)} %bitcast.8, bf16[64,512]{1,0:T(8,128)(2,1)} %q_li.1, bf16[64,512]{1,0:T(8,128)(2,1)} %k_li.1, ...), custom_call_target="tpu_custom_call" | custom-call | tf_op jit(solution)/shard_map/hyena_pair/pallas_call | solution.py:602
  41.2 0.6 %copy.12 = bf16[64,512]{1,0:T(8,128)(2,1)} copy(bf16[64,512]{1,0:T(8,128)(2,1)S(1)} %hyena_pair.1) | data formatting | bytes 131072

commit v3 on v2

--- a/solution.py
+++ b/solution.py
@@ -76,8 +76,6 @@
     y_recv,
     out_sem,
     far_ready,
-    first_ready,
-    ends_ready,
     early_own,
     early,
     first_own,
@@ -107,7 +105,8 @@
     others = [(dz, dc) for dz in range(n_z) for dc in (0, 1) if (dz, dc) != (0, 0)]
     others = others[1:] + others[:1]
 
-    hasty = (z == 2) & (core == 0) if n_z == 4 else None
+    hasty = (z >= 2) & (core == 0) if n_z == 4 else None
+    late = z - 2
 
     def column_sums(gated):
         squares = (gated * gated).T
@@ -139,12 +138,12 @@
             device_id_type=MESH,
         )
 
-    def send_plain(src, dst, sem, dcore):
+    def send_plain(src, dst, sem, dcore, slot):
         return pltpu.make_async_remote_copy(
             src_ref=src,
-            dst_ref=dst,
+            dst_ref=dst.at[slot],
             send_sem=sem.at[dcore],
-            recv_sem=sem.at[2],
+            recv_sem=sem.at[2 + slot],
             device_id={"ctx": plane * group + dcore, "ch": ch},
             device_id_type=MESH,
         )
@@ -173,6 +172,14 @@
     def _():
         for dc in (0, 1):
             greet(in_group(1, dc))
+
+    if n_z == 4:
+
+        @pl.when(z == 0)
+        def _():
+            for place_late in (6, 4):
+                for k in range(n_ch):
+                    greet({"ctx": plane * group + place_late, "ch": lax.rem(ch + k, n_ch)})
 
     greet(in_group(0, 1))
     for k in range(1, n_ch):
@@ -258,6 +265,8 @@
     greeted = n_ch - 1 + n_y - 1 + 1
     greeted += jnp.where(z > 0, 2, 0) + jnp.where(z < n_z - 1, 2, 0)
     greeted += jnp.where((place == group - 1) & (plane < n_y - 1), 1, 0)
+    if n_z == 4:
+        greeted += jnp.where(hasty, 2 * n_ch, 0)
     pl.semaphore_wait(barrier, greeted)
 
     def send_rim():
@@ -279,15 +288,9 @@
 
     if n_z == 4:
 
-        @pl.when(z == 0)
-        def _():
-            tell(first_ready, 1, 0)
-
         @pl.when(z == 1)
         def _():
-            pl.semaphore_wait(first_ready, 1)
             tell(far_ready, 1, 0)
-            tell(ends_ready, 1, core)
 
         @pl.when(z == 2)
         def _():
@@ -348,16 +351,15 @@
 
         @pl.when(hasty)
         def _():
-            pl.semaphore_wait(ends_ready, 2)
             first_own[...] = mine[:1, :TAPS]
             for dcore in (0, 1):
                 for k in range(n_ch):
-                    send_first(dcore, lax.rem(ch + k, n_ch), ch).start()
+                    send_first(dcore, lax.rem(ch + k, n_ch), late * n_ch + ch).start()
             raised_own[...] = jnp.where(
                 first_half, raised[:CHANS], pltpu.roll(raised[CHANS:TAPS], CHANS, 1)
             ).astype(BF16)
             for dcore in (0, 1):
-                send_plain(raised_own, raised_in, raised_sem, dcore).start()
+                send_plain(raised_own, raised_in, raised_sem, dcore, late).start()
 
     if n_z == 4:
 
@@ -425,7 +427,7 @@
             ends = ends_of(v)
             main_own[...] = joined(jnp.where(first_half, ends * decay_half, ends))
             for dcore in (0, 1):
-                send_plain(main_own, main_in, main_sem, dcore).start()
+                send_plain(main_own, main_in, main_sem, dcore, late).start()
 
     for k in range(1, n_ch):
         peer = lax.rem(ch + k, n_ch)
@@ -460,10 +462,12 @@
     def for_others(act, sending):
         for step in others:
             peer = at(*step)
-            if n_z == 4 and step[0] == 2:
-                skip_it = hasty if sending else (z == 0) & (lax.rem(peer, 2) == 0)
-
-                @pl.when(jnp.logical_not(skip_it))
+            if n_z == 4 and step[0] > 0:
+                replaced = (
+                    hasty & (peer < 2) if sending else (z == 0) & (peer >= 4) & (lax.rem(peer, 2) == 0)
+                )
+
+                @pl.when(jnp.logical_not(replaced))
                 def _(peer=peer):
                     act(send_z(peer, place if sending else peer))
 
@@ -496,25 +500,26 @@
 
         @pl.when(z == 0)
         def _():
-            for k in range(n_ch):
-                send_first(0, k, k).wait_recv()
-            total = first[0]
-            for k in range(1, n_ch):
-                total = total + first[k]
-            inv = lax.rsqrt(total / (n_ch * CHANS) + 1e-05)
-            inv_t = jnp.concatenate(
-                [
-                    jnp.broadcast_to(inv, (CHANS, LANES)),
-                    jnp.broadcast_to(pltpu.roll(inv, CHANS, 1), (CHANS, LANES)),
-                ],
-                axis=0,
-            ).T[:CHANS]
-            send_plain(raised_own, raised_in, raised_sem, 0).wait_recv()
-            v = (raised_in[...].astype(F32) * inv_t * gain_row).astype(BF16).astype(F32)
-            age = jnp.where(first_half, float(ROWS - CHANS), float(ROWS - TAPS))
-            added = joined(ends_of(v) * jnp.exp(-rate * age))
-            send_plain(main_own, main_in, main_sem, 0).wait_recv()
-            states_z[4] = main_in[...] + added
+            for slot in (1, 0):
+                for k in range(n_ch):
+                    send_first(0, k, slot * n_ch + k).wait_recv()
+                total = first[slot * n_ch]
+                for k in range(1, n_ch):
+                    total = total + first[slot * n_ch + k]
+                inv = lax.rsqrt(total / (n_ch * CHANS) + 1e-05)
+                inv_t = jnp.concatenate(
+                    [
+                        jnp.broadcast_to(inv, (CHANS, LANES)),
+                        jnp.broadcast_to(pltpu.roll(inv, CHANS, 1), (CHANS, LANES)),
+                    ],
+                    axis=0,
+                ).T[:CHANS]
+                send_plain(raised_own, raised_in, raised_sem, 0, slot).wait_recv()
+                v = (raised_in[slot].astype(F32) * inv_t * gain_row).astype(BF16).astype(F32)
+                age = jnp.where(first_half, float(ROWS - CHANS), float(ROWS - TAPS))
+                added = joined(ends_of(v) * jnp.exp(-rate * age))
+                send_plain(main_own, main_in, main_sem, 0, slot).wait_recv()
+                states_z[4 + 2 * slot] = main_in[slot] + added
 
     for_others(lambda copy: copy.wait_recv(), False)
     run = jnp.zeros((8, LANES), F32)
@@ -581,9 +586,9 @@
                 send_early(lax.rem(ch + k, n_ch), ch).wait_send()
             for dcore in (0, 1):
                 for k in range(n_ch):
-                    send_first(dcore, lax.rem(ch + k, n_ch), ch).wait_send()
-                send_plain(raised_own, raised_in, raised_sem, dcore).wait_send()
-                send_plain(main_own, main_in, main_sem, dcore).wait_send()
+                    send_first(dcore, lax.rem(ch + k, n_ch), late * n_ch + ch).wait_send()
+                send_plain(raised_own, raised_in, raised_sem, dcore, late).wait_send()
+                send_plain(main_own, main_in, main_sem, dcore, late).wait_send()
 
     for k in range(1, n_y):
 
@@ -644,22 +649,20 @@
                 dma((n_y,)),
                 dma,
                 pltpu.SemaphoreType.REGULAR,
-                pltpu.SemaphoreType.REGULAR,
-                pltpu.SemaphoreType.REGULAR,
                 pltpu.VMEM((2, HALF), F32),
                 pltpu.VMEM((n_ch, 2, HALF), F32),
                 pltpu.VMEM((1, TAPS), F32),
-                pltpu.VMEM((n_ch, 1, TAPS), F32),
+                pltpu.VMEM((2 * n_ch, 1, TAPS), F32),
                 pltpu.VMEM((CHANS, LANES), BF16),
-                pltpu.VMEM((CHANS, LANES), BF16),
+                pltpu.VMEM((2, CHANS, LANES), BF16),
                 pltpu.VMEM((8, LANES), F32),
-                pltpu.VMEM((8, LANES), F32),
+                pltpu.VMEM((2, 8, LANES), F32),
                 dma((n_ch,)),
                 dma((n_ch,)),
                 dma((2 * n_ch,)),
-                dma((n_ch,)),
-                dma((3,)),
-                dma((3,)),
+                dma((2 * n_ch,)),
+                dma((4,)),
+                dma((4,)),
             ],
             compiler_params=pltpu.CompilerParams(collective_id=0, has_side_effects=True),
             name="hyena_pair",

time: 42 us -> 41 us (0.976)
  Pallas kernels: 41.2 us -> 40 us
    pallas_call x1, Pallas kernels: 41.2 us -> 40 us  [per_device(): pl.pallas_call(functools.partial(kernel, group), out_shape=pltpu.VMEM((CH...]
where the time goes in v3:
time: 41 us; the launch traced here: 40.7 us
  Pallas kernels  40 us (98%)
  local copies, waits for them, and re-layouts  0.63 us (2%)
    pallas_call x1, Pallas kernels, per_device(): pl.pallas_call(functools.partial(kernel, group), out_shape=pltpu.VMEM((CH...  40 us

profile of v3, /device:TPU:56, one launch (start us, length us, event | category | flops | bytes accessed | tf_op | source)
XLA Modules:
  0.0 40.7 jit_solution(9951420419281089243)
XLA Ops:
  0.0 40.0 %hyena_pair.1 = bf16[64,512]{1,0:T(8,128)(2,1)S(1)} custom-call(bf16[64,512]{1,0:T(8,128)(2,1)} %q_mr.1, bf16[64,512]{1,0:T(8,128)(2,1)} %k_mr.1, bf16[64,512]{1,0:T(8,128)(2,1)} %v_mr.1, bf16[64,128]{1,0:T(8,128)(2,1)} %bitcast.5, f32[1,64]{1,0:T(1,128)} %bitcast.8, bf16[64,512]{1,0:T(8,128)(2,1)} %q_li.1, bf16[64,512]{1,0:T(8,128)(2,1)} %k_li.1, ...), custom_call_target="tpu_custom_call" | custom-call | tf_op jit(solution)/shard_map/hyena_pair/pallas_call | solution.py:607
  40.1 0.6 %copy.12 = bf16[64,512]{1,0:T(8,128)(2,1)} copy(bf16[64,512]{1,0:T(8,128)(2,1)S(1)} %hyena_pair.1) | data formatting | bytes 131072

commit v4 on v3

--- a/solution.py
+++ b/solution.py
@@ -476,21 +476,24 @@
 
     for_others(lambda copy: copy.start(), True)
 
-    inner[...] = skip_row * v
-    block = 64
-    for b in range(HALF // block):
-        low = b * block
-
-        def filt_step(i, acc, low=low):
-            base = HALF - 8 * i
-            for p in range(8):
-                acc = acc + vs[pl.ds(base - p, HALF - low), :] * filt[pl.ds(low + 8 * i + p, 1), :]
-            return acc
-
-        inner[low:, :] += lax.fori_loop(
-            0, block // 8, filt_step, jnp.zeros((HALF - low, LANES), F32)
-        )
-    ql_t = packed(in5[4])
+    def own_filter():
+        inner[...] = skip_row * v
+        block = 64
+        for b in range(HALF // block):
+            low = b * block
+
+            def filt_step(i, acc, low=low):
+                base = HALF - 8 * i
+                for p in range(8):
+                    acc = acc + vs[pl.ds(base - p, HALF - low), :] * filt[pl.ds(low + 8 * i + p, 1), :]
+                return acc
+
+            inner[low:, :] += lax.fori_loop(
+                0, block // 8, filt_step, jnp.zeros((HALF - low, LANES), F32)
+            )
+
+    waited_for = (plane > 0) & (plane < n_y - 1)
+    pl.when(jnp.logical_not(waited_for))(own_filter)
     rate_folded = folded(rate)
     decay_one = jnp.exp(rate_folded * -float(ROWS))
     decay_plane = jnp.exp(rate_folded * -float(ROWS * group))
@@ -545,6 +548,8 @@
         def _(k=k):
             send_y(plane + k, plane).start()
 
+    pl.when(waited_for)(own_filter)
+    ql_t = packed(in5[4])
     for k in range(1, n_y):
 
         @pl.when(plane - k >= 0)

time: 41 us -> 40.5 us (0.988)
  no operation moved by 1% of the time
where the time goes in v4:
time: 40.5 us; the launch traced here: 40.3 us
  Pallas kernels  39.7 us (98%)
  local copies, waits for them, and re-layouts  0.63 us (2%)
    pallas_call x1, Pallas kernels, per_device(): pl.pallas_call(functools.partial(kernel, group), out_shape=pltpu.VMEM((CH...  39.7 us

profile of v4, /device:TPU:56, one launch (start us, length us, event | category | flops | bytes accessed | tf_op | source)
XLA Modules:
  0.0 40.3 jit_solution(2480306160221605710)
XLA Ops:
  0.0 39.7 %hyena_pair.1 = bf16[64,512]{1,0:T(8,128)(2,1)S(1)} custom-call(bf16[64,512]{1,0:T(8,128)(2,1)} %q_mr.1, bf16[64,512]{1,0:T(8,128)(2,1)} %k_mr.1, bf16[64,512]{1,0:T(8,128)(2,1)} %v_mr.1, bf16[64,128]{1,0:T(8,128)(2,1)} %bitcast.5, f32[1,64]{1,0:T(1,128)} %bitcast.8, bf16[64,512]{1,0:T(8,128)(2,1)} %q_li.1, bf16[64,512]{1,0:T(8,128)(2,1)} %k_li.1, ...), custom_call_target="tpu_custom_call" | custom-call | tf_op jit(solution)/shard_map/hyena_pair/pallas_call | solution.py:612
  39.7 0.6 %copy.12 = bf16[64,512]{1,0:T(8,128)(2,1)} copy(bf16[64,512]{1,0:T(8,128)(2,1)S(1)} %hyena_pair.1) | data formatting | bytes 131072

commit v5 on v4

--- a/solution.py
+++ b/solution.py
@@ -343,8 +343,6 @@
             device_id_type=MESH,
         )
 
-    for k in range(1, n_ch):
-        send_sums(lax.rem(ch + k, n_ch), ch).start()
     raised = k_t * gated
 
     if n_z == 4:
@@ -360,6 +358,9 @@
             ).astype(BF16)
             for dcore in (0, 1):
                 send_plain(raised_own, raised_in, raised_sem, dcore, late).start()
+
+    for k in range(1, n_ch):
+        send_sums(lax.rem(ch + k, n_ch), ch).start()
 
     if n_z == 4:
 

time: 40.5 us -> 40.4 us (level)
  no operation moved by 1% of the time
where the time goes in v5:
time: 40.4 us; the launch traced here: 40.2 us
  Pallas kernels  39.6 us (98%)
  local copies, waits for them, and re-layouts  0.63 us (2%)
    pallas_call x1, Pallas kernels, per_device(): pl.pallas_call(functools.partial(kernel, group), out_shape=pltpu.VMEM((CH...  39.6 us

profile of v5, /device:TPU:56, one launch (start us, length us, event | category | flops | bytes accessed | tf_op | source)
XLA Modules:
  0.0 40.2 jit_solution(17637188936699468325)
XLA Ops:
  0.0 39.6 %hyena_pair.1 = bf16[64,512]{1,0:T(8,128)(2,1)S(1)} custom-call(bf16[64,512]{1,0:T(8,128)(2,1)} %q_mr.1, bf16[64,512]{1,0:T(8,128)(2,1)} %k_mr.1, bf16[64,512]{1,0:T(8,128)(2,1)} %v_mr.1, bf16[64,128]{1,0:T(8,128)(2,1)} %bitcast.5, f32[1,64]{1,0:T(1,128)} %bitcast.8, bf16[64,512]{1,0:T(8,128)(2,1)} %q_li.1, bf16[64,512]{1,0:T(8,128)(2,1)} %k_li.1, ...), custom_call_target="tpu_custom_call" | custom-call | tf_op jit(solution)/shard_map/hyena_pair/pallas_call | solution.py:613
  39.6 0.6 %copy.12 = bf16[64,512]{1,0:T(8,128)(2,1)} copy(bf16[64,512]{1,0:T(8,128)(2,1)S(1)} %hyena_pair.1) | data formatting | bytes 131072
